TPU v7x, 256 devices: a whole 4x4x8 slice. The times are simulated.
256 devices in a mesh: src: 32 (over y, z), dst: 8 (over x, core).
Axes of the slice: x: 4, y: 4, z: 8, core: 2. Of those that a mesh axis runs over, the one named last changes fastest.
Arguments:
- transition: bfloat16 [16384, 16384], P('src', 'dst'), may hold values from 5.4931641e-06 to 0.05
- emission: bfloat16 [8192, 16384], P('src', 'dst'), may hold values from 0.099609375 to 5
- forward: bfloat16 [3, 256, 16384], P(None, None, 'src'), may hold values from 0.25 to 4
- beta_end: bfloat16 [256, 16384], P(None, 'dst'), may hold values from 0.5 to 2
- scales: float32 [3, 256], replicated, may hold values from 0.5 to 2
- tokens: int32 [3, 256], replicated, may hold values from 0 to 8191
Outputs:
- counts: float32 [16384, 16384], P('src', 'dst')
- beta_first: float32 [256, 16384], P('dst', 'src')
All inputs are finite; a program needn't handle non-finite values.
Results may differ from a plain program's by a relative error of at most 0.00076.
Values may be sent and summed in bfloat16 or wider, within the bound.
A program may use at most 64 MiB of HBM per device.

v0:
```python
import jax
import jax.numpy as jnp
from jax import lax
from jax.sharding import PartitionSpec as P

B = 256
STEPS = 3


def local_rows(words, emission, first_word):
    keys = words - first_word
    table = (keys[:, None] == jnp.arange(emission.shape[0], dtype=jnp.int32)[None, :]).astype(
        jnp.bfloat16
    )
    return jnp.dot(table, emission, preferred_element_type=jnp.bfloat16)


def emitted_window(words, emission, first_word):
    return (
        lax.psum(local_rows(words, emission, first_word), "src")
        .astype(jnp.float32)
        .astype(jnp.bfloat16)
    )


def per_device(transition, emission, forward, beta_end, scales, tokens):
    steps = forward.shape[0]
    batch = forward.shape[1]
    src_cols = transition.shape[0]
    dst_cols = transition.shape[1]
    n_dst = lax.axis_size("dst")
    share = batch // n_dst
    first_word = lax.axis_index("src") * emission.shape[0]
    emitted_all = emitted_window(tokens.reshape(-1), emission, first_word).reshape(
        steps, batch, dst_cols
    )
    message = beta_end
    pairs = jnp.zeros((src_cols, dst_cols), jnp.float32)
    beta_first = jnp.zeros((share, src_cols), jnp.float32)
    for step in range(steps - 1, -1, -1):
        emitted = emitted_all[step]
        weighted = (
            emitted.astype(jnp.float32) * message.astype(jnp.float32) / scales[step][:, None]
        ).astype(jnp.bfloat16)
        pairs = pairs + lax.dot_general(
            forward[step], weighted, (((0,), (0,)), ((), ())), preferred_element_type=jnp.float32
        )
        partial_rows = lax.dot_general(
            weighted, transition, (((1,), (1,)), ((), ())), preferred_element_type=jnp.float32
        )
        summed = lax.psum(partial_rows, "dst")
        if step == 0:
            beta_first = lax.dynamic_slice_in_dim(summed, lax.axis_index("dst") * share, share, 0)
        else:
            gathered = lax.all_gather(summed.astype(jnp.bfloat16), "src", axis=1, tiled=True)
            message = lax.dynamic_slice_in_dim(
                gathered, lax.axis_index("dst") * dst_cols, dst_cols, 1
            )
    counts = transition.astype(jnp.float32) * pairs * (32.0 / (STEPS * B))
    return (counts, beta_first)


def solution(mesh):
    in_specs = (P("src", "dst"), P("src", "dst"), P(None, None, "src"), P(None, "dst"), P(), P())
    out_specs = (P("src", "dst"), P("dst", "src"))
    return jax.shard_map(
        per_device, mesh=mesh, in_specs=in_specs, out_specs=out_specs, check_vma=False
    )
```

profile of v0, /device:TPU:8, one launch (start us, length us, event | category | flops | bytes accessed | tf_op | source)
XLA Modules:
  0.0 517.3 jit_solution(17679597140141207824)
XLA Ops:
  7.2 0.0 copy-start
  7.2 0.0 all-reduce.5.cloned.1.call-start
  7.2 0.8 broadcast_subtract_fusion
  8.0 0.4 copy-done
  8.4 2.7 fusion.1
  11.1 0.0 copy-start.7
  11.1 0.0 all-reduce.5.cloned.1.call-update
  11.1 0.0 copy-start.5
  11.1 0.0 all-gather.3.cloned.1.call-start
  11.2 0.6 copy-done.7
  11.8 160.7 %all-reduce.5.cloned.1.call-done = bf16[768,2048]{1,0:T(8,128)(2,1)} async-done(((bf16[768,2048]{1,0:T(8,128)(2,1)}), bf16[768,2048]{1,0:T(8,128)(2,1)}) %all-reduce.5.cloned.1.call-update) | async-done | bytes 3145744 | tf_op jit(solution)/shard_map/psum | solution.py:20
  172.5 2.0 divide_convert_fusion.2
  174.4 0.0 copy-start.1
  174.4 1.0 copy-done.1
  175.5 0.0 copy-done.5
  175.5 1.5 fusion.12
  177.0 30.2 %all-reduce.8 = bf16[256,512]{1,0:T(8,128)(2,1)} all-reduce(f32[256,512]{1,0:T(8,128)} %fusion.12), channel_id=1, replica_groups=mesh['src'=32,'dst'=8] {'dst'}, use_global_device_ids=true, to_apply=%region_1.0 | all-reduce | flops 131072 | bytes 786432 | tf_op jit(solution)/shard_map/psum | solution.py:51
  207.2 0.0 all-gather.3.cloned.1.call-update
  207.2 0.0 all-gather.5.cloned.1.call-start
  207.3 98.0 %all-gather.3.cloned.1.call-done = bf16[256,16384]{1,0:T(8,128)(2,1)} async-done(((bf16[256,512]{1,0:T(8,128)(2,1)}), bf16[256,16384]{1,0:T(8,128)(2,1)}) %all-gather.3.cloned.1.call-update) | async-done | bytes 8388624 | tf_op jit(solution)/shard_map/all_gather | solution.py:55
  305.3 2.0 divide_convert_fusion.1
  307.2 0.0 copy-start.2
  307.2 0.9 copy-done.2
  308.2 1.5 fusion.13
  309.7 30.2 %all-reduce.9 = bf16[256,512]{1,0:T(8,128)(2,1)} all-reduce(f32[256,512]{1,0:T(8,128)} %fusion.13), channel_id=1, replica_groups=mesh['src'=32,'dst'=8] {'dst'}, use_global_device_ids=true, to_apply=%region_2.0 | all-reduce | flops 131072 | bytes 786432 | tf_op jit(solution)/shard_map/psum | solution.py:51
  339.9 0.0 all-gather.5.cloned.1.call-update
  339.9 0.0 all-reduce.7.cloned.1.call-start
  340.0 2.9 copy.8
  342.8 0.0 copy-start.3
  342.9 4.1 fusion.6
  347.0 0.0 copy-done.3
  347.0 3.7 fusion.4
  350.6 88.1 %all-gather.5.cloned.1.call-done = bf16[256,16384]{1,0:T(8,128)(2,1)} async-done(((bf16[256,512]{1,0:T(8,128)(2,1)}), bf16[256,16384]{1,0:T(8,128)(2,1)}) %all-gather.5.cloned.1.call-update) | async-done | bytes 8388624 | tf_op jit(solution)/shard_map/all_gather | solution.py:55
  438.8 0.0 copy-start.6
  438.8 2.1 divide_convert_fusion
  440.9 0.0 copy-start.4
  440.9 1.0 copy-done.4
  441.9 0.0 copy-done.6
  441.9 1.5 fusion.14
  443.4 0.0 all-reduce.7.cloned.1.call-update
  443.4 6.9 %fusion = f32[512,2048]{0,1:T(8,128)} fusion(f32[2048,512]{1,0:T(8,128)} %fusion.6, f32[2048,512]{1,0:T(8,128)} %fusion.4, bf16[512,2048]{0,1:T(8,128)(2,1)S(1)} %copy.8, bf16[256,2048]{1,0:T(8,128)(2,1)} %copy-done.4, bf16[3,256,512]{2,1,0:T(8,128)(2,1)} %param.8), kind=kOutput, calls=%fused_computation.1 | convolution fusion | flops 542113792 | bytes 15990784 | tf_op jit(solution)/shard_map/dot_general | solution.py:45
  450.3 5.3 %copy.9 = f32[512,2048]{1,0:T(8,128)} copy(f32[512,2048]{0,1:T(8,128)} %fusion) | data formatting | bytes 8388608
  455.7 53.7 %all-reduce.7.cloned.1.call-done = f32[256,512]{1,0:T(8,128)} async-done(((f32[256,512]{1,0:T(8,128)}), f32[256,512]{1,0:T(8,128)}) %all-reduce.7.cloned.1.call-update) | async-done | bytes 524304 | tf_op jit(solution)/shard_map/psum | solution.py:51
  509.3 1.5 constant_dynamic-slice_fusion
  (2 shorter events, 0.0 us)
Async XLA Ops:
  7.2 1.2 copy-start
  7.2 165.3 %all-reduce.5.cloned.1.call-start = ((), (), s32[]{:S(2)}) async-start(), calls=%async_computation | async-start | bytes 6291456 | tf_op jit(solution)/shard_map/psum | solution.py:20
  11.1 0.7 copy-start.7
  11.1 164.4 %copy-start.5 = (bf16[512,2048]{1,0:T(8,128)(2,1)S(1)}, bf16[512,2048]{1,0:T(8,128)(2,1)}, u32[]{:S(2)}) copy-start(bf16[512,2048]{1,0:T(8,128)(2,1)} %param.6) | copy-start | bytes 6291460
  11.1 294.1 %all-gather.3.cloned.1.call-start = ((), (), s32[]{:S(2)}) async-start(), calls=%async_computation.1 | async-start | bytes 8650752 | tf_op jit(solution)/shard_map/all_gather | solution.py:55
  174.4 1.1 copy-start.1
  207.2 231.5 %all-gather.5.cloned.1.call-start = ((), (), s32[]{:S(2)}) async-start(), calls=%async_computation.2 | async-start | bytes 8650752 | tf_op jit(solution)/shard_map/all_gather | solution.py:55
  307.2 1.0 copy-start.2
  339.9 169.4 %all-reduce.7.cloned.1.call-start = ((), (), s32[]{:S(2)}) async-start(), calls=%async_computation.3 | async-start | bytes 1048576 | tf_op jit(solution)/shard_map/psum | solution.py:51
  342.8 4.1 copy-start.3
  438.8 3.1 copy-start.6
  440.9 1.0 copy-start.4
Sparse Core Ops, SparseCore 0:
  12.1 160.3 all-reduce.4
  207.4 97.8 all-gather.2
  340.0 98.6 all-gather.4
  443.5 65.7 all-reduce.6
where the time goes:
time: 518 us; the launch traced here: 517 us
  waiting for transfers between devices  400 us (77%)
  blocking collectives  60.3 us (12%)
  matrix products  22 us (4%)
  between operations  13.9 us (3%)
  local copies, waits for them, and re-layouts  13.7 us (3%)
  other arithmetic  6.79 us (1%)
    all_gather x2, waiting for transfers between devices, per_device(): lax.all_gather(summed.astype(jnp.bfloat16), 'src', axis=1, tiled=True)  186 us
    psum x1, waiting for transfers between devices, emitted_window(): lax.psum(local_rows(words, emission, first_word), 'src').astype(jnp.float32)  161 us
    psum x2, blocking collectives, per_device(): summed = lax.psum(partial_rows, 'dst')  60.3 us
    psum x1, waiting for transfers between devices, per_device(): summed = lax.psum(partial_rows, 'dst')  53.7 us
    dot_general x3, matrix products, per_device(): lax.dot_general(forward[step], weighted, (((0,), (0,)), ((), ())), prefer...  14.7 us
    unnamed x18, local copies, waits for them, and re-layouts  12.2 us
  transfers between devices with their start and end apart: 4, of which 4 were waited for; matrix products, arithmetic and copies ran while one was open for 4% of the time, Pallas kernels for 0%

commit v1 on v0

--- a/solution.py
+++ b/solution.py
@@ -48,7 +48,11 @@
         partial_rows = lax.dot_general(
             weighted, transition, (((1,), (1,)), ((), ())), preferred_element_type=jnp.float32
         )
-        summed = lax.psum(partial_rows, "dst")
+        size = lax.axis_size("dst")
+        summed, far = (partial_rows, 1)
+        while far < size:
+            summed = summed + lax.ppermute(summed, "dst", [(i, i ^ far) for i in range(size)])
+            far = 2 * far
         if step == 0:
             beta_first = lax.dynamic_slice_in_dim(summed, lax.axis_index("dst") * share, share, 0)
         else:

time: 518 us -> 492 us (0.950)
  blocking collectives: 60.3 us -> 0 us
  waiting for transfers between devices: 400 us -> 429 us
  starting transfers between devices: 0.16 us -> 14.1 us
  matrix products: 22 us -> 11.2 us
  other arithmetic: 6.79 us -> 12.3 us
    ppermute x0 -> x9, waiting for transfers between devices: none -> 66.4 us  [per_device(): lax.ppermute(summed, 'dst', [(i, i ^ far) for i in range(size)])]
    psum x2 -> x0, blocking collectives: 60.3 us -> none  [per_device(): summed = lax.psum(partial_rows, 'dst')]
    psum x1 -> x0, waiting for transfers between devices: 53.7 us -> none  [per_device(): summed = lax.psum(partial_rows, 'dst')]
    all_gather x2, waiting for transfers between devices: 186 us -> 202 us  [per_device(): lax.all_gather(summed.astype(jnp.bfloat16), 'src', axis=1, tiled=True)]
    ppermute x0 -> x9, starting transfers between devices: none -> 14 us  [per_device(): lax.ppermute(summed, 'dst', [(i, i ^ far) for i in range(size)])]
    dot_general x3, matrix products: 14.7 us -> 5.44 us  [per_device(): lax.dot_general(forward[step], weighted, (((0,), (0,)), ((), ())), prefer...]
    unnamed x18 -> x22, local copies, waits for them, and re-layouts: 12.2 us -> 10.3 us
  transfers between devices with their start and end apart: 4 -> 12, of which waited for: 4 -> 11; matrix products, arithmetic and copies ran while one was open for 4% -> 3% of each run, Pallas kernels for 0% -> 0%
where the time goes in v1:
time: 492 us; the launch traced here: 491 us
  waiting for transfers between devices  429 us (87%)
  starting transfers between devices  14.1 us (3%)
  between operations  14 us (3%)
  other arithmetic  12.3 us (2%)
  matrix products  11.2 us (2%)
  local copies, waits for them, and re-layouts  10.3 us (2%)
    all_gather x2, waiting for transfers between devices, per_device(): lax.all_gather(summed.astype(jnp.bfloat16), 'src', axis=1, tiled=True)  202 us
    psum x1, waiting for transfers between devices, emitted_window(): lax.psum(local_rows(words, emission, first_word), 'src').astype(jnp.float32)  161 us
    ppermute x9, waiting for transfers between devices, per_device(): lax.ppermute(summed, 'dst', [(i, i ^ far) for i in range(size)])  66.4 us
    ppermute x9, starting transfers between devices, per_device(): lax.ppermute(summed, 'dst', [(i, i ^ far) for i in range(size)])  14 us
    unnamed x22, local copies, waits for them, and re-layouts  10.3 us
  transfers between devices with their start and end apart: 12, of which 11 were waited for; matrix products, arithmetic and copies ran while one was open for 3% of the time, Pallas kernels for 0%

profile of v1, /device:TPU:8, one launch (start us, length us, event | category | flops | bytes accessed | tf_op | source)
XLA Modules:
  0.0 490.5 jit_solution(15180645733023756691)
XLA Ops:
  7.2 0.0 all-reduce.2.cloned.1.call-start
  7.2 0.8 broadcast_subtract_fusion
  8.0 0.4 copy-done
  8.4 2.7 fusion.1
  11.1 0.0 all-reduce.2.cloned.1.call-update
  11.1 0.0 all-gather.3.cloned.1.call-start
  11.2 0.6 copy-done.9
  11.8 160.7 %all-reduce.2.cloned.1.call-done = bf16[768,2048]{1,0:T(8,128)(2,1)} async-done(((bf16[768,2048]{1,0:T(8,128)(2,1)}), bf16[768,2048]{1,0:T(8,128)(2,1)}) %all-reduce.2.cloned.1.call-update) | async-done | bytes 3145744 | tf_op jit(solution)/shard_map/psum | solution.py:20
  172.5 2.0 divide_convert_fusion.2
  174.5 0.7 fusion.12
  175.2 0.1 collective-permute-start
  175.3 1.9 collective-permute-done
  177.2 0.1 add.46
  177.3 1.6 collective-permute-start.1
  178.8 12.5 %collective-permute-done.1 = f32[256,512]{1,0:T(8,128)S(1)} collective-permute-done((f32[256,512]{1,0:T(8,128)S(1)}, f32[256,512]{1,0:T(8,128)S(1)}, u32[]{:S(2)}, u32[]{:S(2)}) %collective-permute-start.1) | collective-permute-done | bytes 524320 | tf_op jit(solution)/shard_map/ppermute | solution.py:54
  191.4 0.1 add.47
  191.4 3.1 collective-permute-start.2
  194.5 11.6 %collective-permute-done.2 = f32[256,512]{1,0:T(8,128)S(1)} collective-permute-done((f32[256,512]{1,0:T(8,128)S(1)}, f32[256,512]{1,0:T(8,128)S(1)}, u32[]{:S(2)}, u32[]{:S(2)}) %collective-permute-start.2) | collective-permute-done | bytes 524320 | tf_op jit(solution)/shard_map/ppermute | solution.py:54
  206.1 0.8 add_convert_fusion.1
  206.9 0.0 all-gather.5.cloned.1.call-start
  207.0 100.3 %all-gather.3.cloned.1.call-done = bf16[256,16384]{1,0:T(8,128)(2,1)} async-done(((bf16[256,512]{1,0:T(8,128)(2,1)}), bf16[256,16384]{1,0:T(8,128)(2,1)}) %all-gather.3.cloned.1.call-update) | async-done | bytes 8388624 | tf_op jit(solution)/shard_map/all_gather | solution.py:59
  307.3 2.0 divide_convert_fusion.1
  309.3 0.7 fusion.13
  310.0 0.1 collective-permute-start.3
  310.1 1.9 collective-permute-done.3
  312.0 0.1 add.51
  312.1 1.6 collective-permute-start.4
  313.7 12.5 %collective-permute-done.4 = f32[256,512]{1,0:T(8,128)S(1)} collective-permute-done((f32[256,512]{1,0:T(8,128)S(1)}, f32[256,512]{1,0:T(8,128)S(1)}, u32[]{:S(2)}, u32[]{:S(2)}) %collective-permute-start.4) | collective-permute-done | bytes 524320 | tf_op jit(solution)/shard_map/ppermute | solution.py:54
  326.2 0.1 add.52
  326.3 3.1 collective-permute-start.5
  329.3 11.6 %collective-permute-done.5 = f32[256,512]{1,0:T(8,128)S(1)} collective-permute-done((f32[256,512]{1,0:T(8,128)S(1)}, f32[256,512]{1,0:T(8,128)S(1)}, u32[]{:S(2)}, u32[]{:S(2)}) %collective-permute-start.5) | collective-permute-done | bytes 524320 | tf_op jit(solution)/shard_map/ppermute | solution.py:54
  341.0 0.8 add_convert_fusion
  341.8 101.2 %all-gather.5.cloned.1.call-done = bf16[256,16384]{1,0:T(8,128)(2,1)} async-done(((bf16[256,512]{1,0:T(8,128)(2,1)}), bf16[256,16384]{1,0:T(8,128)(2,1)}) %all-gather.5.cloned.1.call-update) | async-done | bytes 8388624 | tf_op jit(solution)/shard_map/all_gather | solution.py:59
  443.0 2.0 divide_convert_fusion
  445.0 1.0 copy-done.5
  446.0 1.6 fusion.14
  447.6 2.9 copy.8
  450.5 1.4 add.56
  451.9 1.6 collective-permute-start.7
  453.4 1.7 fusion.6
  455.1 0.7 fusion.4
  455.9 10.4 %collective-permute-done.7 = f32[256,512]{1,0:T(8,128)S(1)} collective-permute-done((f32[256,512]{1,0:T(8,128)S(1)}, f32[256,512]{1,0:T(8,128)S(1)}, u32[]{:S(2)}, u32[]{:S(2)}) %collective-permute-start.7) | collective-permute-done | bytes 524320 | tf_op jit(solution)/shard_map/ppermute | solution.py:54
  466.3 0.9 add.57
  467.2 3.0 collective-permute-start.8
  470.2 3.0 fusion
  473.2 5.3 %copy.9 = f32[512,2048]{1,0:T(8,128)} copy(f32[512,2048]{0,1:T(8,128)} %fusion) | data formatting | bytes 8388608
  478.5 4.0 collective-permute-done.8
  482.5 1.5 dynamic-slice_add_fusion
  (23 shorter events, 0.1 us)
Async XLA Ops:
  7.2 1.2 copy-start
  7.2 165.3 %all-reduce.2.cloned.1.call-start = ((), (), s32[]{:S(2)}) async-start(), calls=%async_computation | async-start | bytes 6291456 | tf_op jit(solution)/shard_map/psum | solution.py:20
  11.1 0.7 copy-start.9
  11.1 163.3 %copy-start.7 = (bf16[512,2048]{1,0:T(8,128)(2,1)S(1)}, bf16[512,2048]{1,0:T(8,128)(2,1)}, u32[]{:S(2)}) copy-start(bf16[512,2048]{1,0:T(8,128)(2,1)} %param.6) | copy-start | bytes 6291460
  11.1 296.2 %all-gather.3.cloned.1.call-start = ((), (), s32[]{:S(2)}) async-start(), calls=%async_computation.1 | async-start | bytes 8650752 | tf_op jit(solution)/shard_map/all_gather | solution.py:59
  174.4 2.8 copy-start.1
  175.2 2.0 collective-permute-start
  177.3 14.1 %collective-permute-start.1 = (f32[256,512]{1,0:T(8,128)S(1)}, f32[256,512]{1,0:T(8,128)S(1)}, u32[]{:S(2)}, u32[]{:S(2)}) collective-permute-start(f32[256,512]{1,0:T(8,128)S(1)} %add.46), channel_id=1, source_target_pairs={{0,2},{1,3},{2,0},{3,1},{4,6},{5,7},{6,4},{7,5},{8,10},{9,11},{10,... | collective-permute-start | bytes 1572872 | tf_op jit(solution)/shard_map/ppermute | solution.py:54
  191.4 14.7 %collective-permute-start.2 = (f32[256,512]{1,0:T(8,128)S(1)}, f32[256,512]{1,0:T(8,128)S(1)}, u32[]{:S(2)}, u32[]{:S(2)}) collective-permute-start(f32[256,512]{1,0:T(8,128)S(1)} %add.47), channel_id=1, source_target_pairs={{0,4},{1,5},{2,6},{3,7},{4,0},{5,1},{6,2},{7,3},{8,12},{9,13},{10,... | collective-permute-start | bytes 1572872 | tf_op jit(solution)/shard_map/ppermute | solution.py:54
  206.9 236.1 %all-gather.5.cloned.1.call-start = ((), (), s32[]{:S(2)}) async-start(), calls=%async_computation.2 | async-start | bytes 8650752 | tf_op jit(solution)/shard_map/all_gather | solution.py:59
  309.3 2.9 copy-start.3
  310.0 2.0 collective-permute-start.3
  312.1 14.1 %collective-permute-start.4 = (f32[256,512]{1,0:T(8,128)S(1)}, f32[256,512]{1,0:T(8,128)S(1)}, u32[]{:S(2)}, u32[]{:S(2)}) collective-permute-start(f32[256,512]{1,0:T(8,128)S(1)} %add.51), channel_id=1, source_target_pairs={{0,2},{1,3},{2,0},{3,1},{4,6},{5,7},{6,4},{7,5},{8,10},{9,11},{10,... | collective-permute-start | bytes 1572872 | tf_op jit(solution)/shard_map/ppermute | solution.py:54
  326.3 14.7 %collective-permute-start.5 = (f32[256,512]{1,0:T(8,128)S(1)}, f32[256,512]{1,0:T(8,128)S(1)}, u32[]{:S(2)}, u32[]{:S(2)}) collective-permute-start(f32[256,512]{1,0:T(8,128)S(1)} %add.52), channel_id=1, source_target_pairs={{0,4},{1,5},{2,6},{3,7},{4,0},{5,1},{6,2},{7,3},{8,12},{9,13},{10,... | collective-permute-start | bytes 1572872 | tf_op jit(solution)/shard_map/ppermute | solution.py:54
  445.0 1.0 copy-start.5
  447.6 2.9 collective-permute-start.6
  450.4 3.0 copy-start.2
  451.8 3.3 copy-start.4
  451.8 3.3 copy-start.8
  451.9 14.4 %collective-permute-start.7 = (f32[256,512]{1,0:T(8,128)S(1)}, f32[256,512]{1,0:T(8,128)S(1)}, u32[]{:S(2)}, u32[]{:S(2)}) collective-permute-start(f32[256,512]{1,0:T(8,128)S(1)} %add.56), channel_id=1, source_target_pairs={{0,2},{1,3},{2,0},{3,1},{4,6},{5,7},{6,4},{7,5},{8,10},{9,11},{10,... | collective-permute-start | bytes 1572872 | tf_op jit(solution)/shard_map/ppermute | solution.py:54
  455.9 14.3 %copy-start.6 = (bf16[256,2048]{1,0:T(8,128)(2,1)S(1)}, bf16[256,2048]{1,0:T(8,128)(2,1)}, u32[]{:S(2)}) copy-start(bf16[256,2048]{1,0:T(8,128)(2,1)} %copy-done.5) | copy-start | bytes 3145732
  467.2 15.3 %collective-permute-start.8 = (f32[256,512]{1,0:T(8,128)}, f32[256,512]{1,0:T(8,128)}, u32[]{:S(2)}, u32[]{:S(2)}) collective-permute-start(f32[256,512]{1,0:T(8,128)} %add.57), channel_id=1, source_target_pairs={{0,4},{1,5},{2,6},{3,7},{4,0},{5,1},{6,2},{7,3},{8,12},{9,13},{10,... | collective-permute-start | bytes 1572872 | tf_op jit(solution)/shard_map/ppermute | solution.py:54
Sparse Core Ops, SparseCore 0:
  12.1 160.3 all-reduce.1
  207.0 100.2 all-gather.2
  341.9 101.0 all-gather.4
